TPU v7x, 32 devices: a whole 2x2x4 slice. The times are simulated.
32 devices in a mesh: gx: 16 (over z, y, x), gy: 2 (over core).
Axes of the slice: x: 2, y: 2, z: 4, core: 2. Of those that a mesh axis runs over, the one named last changes fastest.
Arguments:
- observed: float32 [8192, 128], P(('gx', 'gy')), may hold values from -6 to 6
- jacobian: bfloat16 [8192, 64, 128], P(('gx', 'gy'))
- tile_block: int32 [8192], P(('gx', 'gy')), may hold values from 0 to 127
- params: float32 [128, 64], replicated, may hold values from -3 to 3
- damping: float32 [1], replicated, may hold values from 0.05 to 2
Outputs:
- scaled_step: float32 [128, 64], P('gy')
- misfit: float32 [], replicated
All inputs are finite; a program needn't handle non-finite values.
Results may differ from a plain program's by a relative error of at most 0.0031.
Values sent between devices are 32-bit elements; how exact they have to be, the bound alone decides.
No kernel may reach another device: no remote copies, remote signals or barrier semaphores. Data moves between devices by JAX's collectives and lax.ppermute only.
A program may use at most 64 MiB of HBM per device.

v0:
```python
import jax
import jax.numpy as jnp
from jax import lax
from jax.sharding import PartitionSpec as P

NB = 128


def swapped(value, axis, bit):
    return lax.ppermute(value, axis, [(i, i ^ 1 << bit) for i in range(lax.axis_size(axis))])


def solve_blocks(system, rhs):
    size = system.shape[1]
    augmented = jnp.concatenate([system, rhs[:, :, None]], axis=2)
    augmented = jnp.transpose(augmented, (1, 2, 0))
    row_ids = jnp.arange(size, dtype=jnp.int32)

    def eliminate(step, current):
        column = step.astype(jnp.int32)
        pivot_row = lax.dynamic_index_in_dim(current, column, 0, keepdims=False)
        pivot = lax.dynamic_index_in_dim(pivot_row, column, 0, keepdims=False)
        pivot_row = pivot_row / pivot[None, :]
        factors = lax.dynamic_index_in_dim(current, column, 1, keepdims=False)
        updated = current - factors[:, None, :] * pivot_row[None, :, :]
        is_pivot = (row_ids == column)[:, None, None]
        return jnp.where(is_pivot, pivot_row[None, :, :], updated)

    final = lax.fori_loop(0, size, eliminate, augmented)
    return jnp.transpose(final[:, size, :], (1, 0))


def local(observed, jacobian, tile_block, params, damping):
    moved = observed
    for bit_x in range(lax.axis_size("gx").bit_length() - 1):
        moved = swapped(moved, "gx", bit_x)
    for bit_y in range(lax.axis_size("gy").bit_length() - 1):
        moved = swapped(moved, "gy", bit_y)
    reflected_values = moved[::-1, ::-1]
    block_ids = jnp.arange(NB, dtype=jnp.int32)
    onehot = (tile_block[:, None] == block_ids[None, :]).astype(jnp.float32)
    tile_params = jnp.dot(onehot, params, precision=lax.Precision.HIGHEST).astype(jnp.bfloat16)
    calculated_values = jnp.einsum(
        "tpv,tp->tv", jacobian, tile_params, preferred_element_type=jnp.float32
    )
    residual_values = 0.5 * (observed + reflected_values) - calculated_values
    local_misfit = jnp.sum(residual_values * residual_values)
    resid_b = residual_values.astype(jnp.bfloat16)
    tile_grad = jnp.einsum("tpv,tv->tp", jacobian, resid_b, preferred_element_type=jnp.float32)
    tile_gram = jnp.einsum("tpv,tqv->tpq", jacobian, jacobian, preferred_element_type=jnp.float32)
    gram = jnp.einsum("tb,tpq->bpq", onehot, tile_gram, precision=lax.Precision.HIGHEST)
    grad = jnp.dot(onehot.T, tile_grad, precision=lax.Precision.HIGHEST)
    owned = NB // lax.axis_size("gy")
    gram, grad, total_misfit = lax.psum((gram, grad, local_misfit), ("gx", "gy"))
    leading_entry = lax.axis_index("gy") * owned
    gram = lax.dynamic_slice_in_dim(gram, leading_entry, owned, 0)
    grad = lax.dynamic_slice_in_dim(grad, leading_entry, owned, 0)
    misfit = total_misfit / (
        observed.shape[0] * lax.axis_size("gx") * lax.axis_size("gy") * observed.shape[1]
    )
    diagonal = jnp.diagonal(gram, axis1=1, axis2=2)
    eye = jnp.eye(gram.shape[1], dtype=jnp.float32)
    system = gram + damping[0] * diagonal[:, :, None] * eye[None] + eye[None]
    delta = solve_blocks(system, grad)
    return (delta * jnp.sqrt(diagonal), misfit)


def solution(mesh):
    return jax.shard_map(
        local,
        mesh=mesh,
        in_specs=(P(("gx", "gy"), None), P(("gx", "gy"), None, None), P(("gx", "gy")), P(), P()),
        out_specs=(P("gy", None), P()),
        check_vma=False,
    )
```

profile of v0, /device:TPU:0, one launch (start us, length us, event | category | flops | bytes accessed | tf_op | source)
XLA Modules:
  0.0 237.3 jit_solution(4161908257750440027)
XLA Ops:
  7.2 3.0 %collective-permute-start = (f32[256,128]{1,0:T(8,128)}, f32[256,128]{1,0:T(8,128)S(1)}, u32[]{:S(2)}, u32[]{:S(2)}) collective-permute-start(f32[256,128]{1,0:T(8,128)} %param.7), channel_id=1, source_target_pairs={{0,2},{2,0},{4,6},{6,4},{8,10},{10,8},{12,14},{14,12},{16,18},{18,... | collective-permute-start | bytes 393224 | tf_op jit(solution)/shard_map/ppermute | solution.py:10
  10.3 3.7 %collective-permute-done = f32[256,128]{1,0:T(8,128)S(1)} collective-permute-done((f32[256,128]{1,0:T(8,128)}, f32[256,128]{1,0:T(8,128)S(1)}, u32[]{:S(2)}, u32[]{:S(2)}) %collective-permute-start) | collective-permute-done | bytes 131104 | tf_op jit(solution)/shard_map/ppermute | solution.py:10
  14.0 1.8 collective-permute-start.1
  15.7 5.8 %fusion.21 = f32[256,64,64]{2,1,0:T(8,128)S(1)} fusion(bf16[256,64,128]{2,1,0:T(8,128)(2,1)} %param.8), kind=kOutput, calls=%fused_computation.37 | convolution fusion | flops 268435456 | bytes 8388608 | tf_op jit(solution)/shard_map/tpv,tqv->tpq/dot_general | solution.py:50
  21.5 1.6 collective-permute-start.2
  23.2 10.1 %fusion.3 = f32[128,64,64]{2,0,1:T(8,128)} fusion(f32[256,64,64]{2,1,0:T(8,128)S(1)} %fusion.21, s32[256]{0:T(256)S(1)} %copy-done.2), kind=kOutput, calls=%fused_computation.8 | convolution fusion | flops 1610645504 | bytes 6292480 | tf_op jit(solution)/shard_map/tb,tpq->bpq/dot_general | solution.py:51
  33.6 2.7 %collective-permute-start.3 = (f32[256,128]{1,0:T(8,128)S(1)}, f32[256,128]{1,0:T(8,128)S(1)}, u32[]{:S(2)}, u32[]{:S(2)}) collective-permute-start(f32[256,128]{1,0:T(8,128)S(1)} %collective-permute-done.2), channel_id=1, source_target_pairs={{0,16},{2,18},{4,20},{6,22},{8,24},{10,26},{12,28},{14,30},{16,0},... | collective-permute-start | bytes 393224 | tf_op jit(solution)/shard_map/ppermute | solution.py:10
  36.2 3.7 %fusion.8 = f32[256,1,128]{2,1,0:T(1,128)S(1)} fusion(bf16[256,64,128]{2,1,0:T(8,128)(2,1)} %param.8, bf16[256,64,1]{1,0,2:T(8,128)(2,1)S(1)} %fusion.5), kind=kOutput, calls=%fused_computation.16 | convolution fusion | flops 4194304 | bytes 4358144 | tf_op jit(solution)/shard_map/tpv,tp->tv/dot_general | solution.py:43
  39.9 1.3 collective-permute-done.3
  41.8 0.7 collective-permute-done.4
  42.7 0.6 multiply_reduce_fusion
  43.3 4.6 %fusion.6 = f32[256,1,64]{2,1,0:T(1,128)S(1)} fusion(bf16[256,64,128]{2,1,0:T(8,128)(2,1)} %param.8, bf16[256,128,1]{1,0,2:T(8,128)(2,1)S(1)} %get-tuple-element.124), kind=kOutput, calls=%fused_computation.14 | convolution fusion | flops 4194304 | bytes 4325376 | tf_op jit(solution)/shard_map/tpv,tv->tp/dot_general | solution.py:49
  48.1 40.2 %all-reduce = (f32[128,64]{1,0:T(8,128)S(1)}, f32[]{:T(128)}) all-reduce(f32[128,64]{1,0:T(8,128)S(1)} %fusion.10, f32[]{:T(128)} %get-tuple-element.123), channel_id=1, replica_groups=mesh['gx'=16,'gy'=2] {'gx','gy'}, use_global_device_ids=true, to_apply=%region_1.0 | all-reduce | flops 8193 | bytes 65544 | tf_op jit(solution)/shard_map/psum | solution.py:54
  88.3 1.9 copy.13
  90.9 84.2 %all-reduce.3.cloned.1.call-done = f32[128,64,64]{2,0,1:T(8,128)} async-done(((f32[128,64,64]{2,0,1:T(8,128)}), f32[128,64,64]{2,0,1:T(8,128)}) %all-reduce.3.cloned.1.call-update) | async-done | bytes 2097168 | tf_op jit(solution)/shard_map/psum | solution.py:54
  175.2 3.2 %constant_dynamic-slice_fusion.2 = f32[64,64,64]{2,0,1:T(8,128)} fusion(f32[128,64,64]{2,0,1:T(8,128)} %all-reduce.3.cloned.1.call-done, s32[]{:T(128)S(6)} %select_n.46), kind=kLoop, calls=%fused_computation.36 | loop fusion | bytes 2097156 | tf_op jit(solution)/shard_map/dynamic_slice | solution.py:56
  178.4 2.9 %copy.12 = f32[64,64,64]{0,2,1:T(8,128)} copy(f32[64,64,64]{2,0,1:T(8,128)} %constant_dynamic-slice_fusion.2) | data formatting | bytes 2097152 | tf_op jit(solution)/shard_map/dynamic_slice | solution.py:56
  181.3 1.5 gather_fusion
  182.8 2.0 add_add_fusion
  184.7 2.0 maximum_bitcast_fusion
  186.7 2.2 copy.14
  188.9 39.3 %while.17 = (s32[]{:T(128)}, f32[64,65,64]{2,1,0:T(8,128)S(1)}, s32[]{:T(128)}, s32[]{:T(128)}, s32[]{:T(128)}, /*index=5*/s32[]{:T(128)}) while((s32[]{:T(128)}, f32[64,65,64]{2,1,0:T(8,128)S(1)}, s32[]{:T(128)}, s32[]{:T(128)}, s32[]{:T(128)}, /*index=5*/s32[]{:T(128)}) %tuple.51), condition=%wide.region_3.0_spmd.clone, body=%wide.region_2.0_spmd.clone.sunk | while | flops 802948 | bytes 2230009 | solution.py:29
  189.0 0.5 subtract_select_fusion.2
  189.6 0.5 subtract_select_fusion.2
  190.2 0.5 subtract_select_fusion.2
  190.8 0.5 subtract_select_fusion.2
  191.4 0.5 subtract_select_fusion.2
  192.1 0.5 subtract_select_fusion.2
  192.7 0.5 subtract_select_fusion.2
  193.3 0.5 subtract_select_fusion.2
  193.9 0.5 subtract_select_fusion.2
  194.5 0.5 subtract_select_fusion.2
  195.1 0.5 subtract_select_fusion.2
  195.7 0.5 subtract_select_fusion.2
  196.4 0.5 subtract_select_fusion.2
  197.0 0.5 subtract_select_fusion.2
  197.6 0.5 subtract_select_fusion.2
  198.2 0.5 subtract_select_fusion.2
  198.8 0.5 subtract_select_fusion.2
  199.4 0.5 subtract_select_fusion.2
  200.0 0.5 subtract_select_fusion.2
  200.7 0.5 subtract_select_fusion.2
  201.3 0.5 subtract_select_fusion.2
  201.9 0.5 subtract_select_fusion.2
  202.5 0.5 subtract_select_fusion.2
  203.1 0.5 subtract_select_fusion.2
  203.7 0.5 subtract_select_fusion.2
  205.0 0.5 subtract_select_fusion.2
  206.2 0.5 subtract_select_fusion.2
  207.4 0.5 subtract_select_fusion.2
  208.6 0.5 subtract_select_fusion.2
  211.7 0.5 subtract_select_fusion.2
  212.9 0.5 subtract_select_fusion.2
  214.2 0.5 subtract_select_fusion.2
  215.4 0.5 subtract_select_fusion.2
  216.6 0.5 subtract_select_fusion.2
  217.9 0.5 subtract_select_fusion.2
  219.1 0.5 subtract_select_fusion.2
  220.3 0.5 subtract_select_fusion.2
  223.4 0.5 subtract_select_fusion.2
  224.6 0.5 subtract_select_fusion.2
  225.8 0.5 subtract_select_fusion.2
  227.1 0.5 subtract_select_fusion.2
  228.6 0.7 copy.16
  (299 shorter events, 16.8 us)
Async XLA Ops:
  7.2 26.1 %copy-start = (f32[128,64]{0,1:T(8,128)S(1)}, f32[128,64]{0,1:T(8,128)}, u32[]{:S(2)}) copy-start(f32[128,64]{0,1:T(8,128)} %param.10) | copy-start | bytes 98308
  7.2 16.0 %copy-start.2 = (s32[256]{0:T(256)S(1)}, s32[256]{0:T(256)}, u32[]{:S(2)}) copy-start(s32[256]{0:T(256)} %param.9) | copy-start | bytes 3076
  7.2 168.0 %all-reduce.3.cloned.1.call-start = ((), (), s32[]{:S(2)}) async-start(), calls=%async_computation | async-start | bytes 8388608 | tf_op jit(solution)/shard_map/psum | solution.py:54
  7.2 6.7 %collective-permute-start = (f32[256,128]{1,0:T(8,128)}, f32[256,128]{1,0:T(8,128)S(1)}, u32[]{:S(2)}, u32[]{:S(2)}) collective-permute-start(f32[256,128]{1,0:T(8,128)} %param.7), channel_id=1, source_target_pairs={{0,2},{2,0},{4,6},{6,4},{8,10},{10,8},{12,14},{14,12},{16,18},{18,... | collective-permute-start | bytes 393224 | tf_op jit(solution)/shard_map/ppermute | solution.py:10
  14.0 7.5 %collective-permute-start.1 = (f32[256,128]{1,0:T(8,128)S(1)}, f32[256,128]{1,0:T(8,128)S(1)}, u32[]{:S(2)}, u32[]{:S(2)}) collective-permute-start(f32[256,128]{1,0:T(8,128)S(1)} %collective-permute-done), channel_id=1, source_target_pairs={{0,4},{2,6},{4,0},{6,2},{8,12},{10,14},{12,8},{14,10},{16,20},{18,... | collective-permute-start | bytes 393224 | tf_op jit(solution)/shard_map/ppermute | solution.py:10
  21.5 12.0 %collective-permute-start.2 = (f32[256,128]{1,0:T(8,128)S(1)}, f32[256,128]{1,0:T(8,128)S(1)}, u32[]{:S(2)}, u32[]{:S(2)}) collective-permute-start(f32[256,128]{1,0:T(8,128)S(1)} %collective-permute-done.1), channel_id=1, source_target_pairs={{0,8},{2,10},{4,12},{6,14},{8,0},{10,2},{12,4},{14,6},{16,24},{18,... | collective-permute-start | bytes 393224 | tf_op jit(solution)/shard_map/ppermute | solution.py:10
  33.6 9.1 %copy-start.1 = (f32[256,128]{1,0:T(8,128)S(1)}, f32[256,128]{1,0:T(8,128)}, u32[]{:S(2)}) copy-start(f32[256,128]{1,0:T(8,128)} %param.7) | copy-start | bytes 393220
  33.6 7.6 %collective-permute-start.3 = (f32[256,128]{1,0:T(8,128)S(1)}, f32[256,128]{1,0:T(8,128)S(1)}, u32[]{:S(2)}, u32[]{:S(2)}) collective-permute-start(f32[256,128]{1,0:T(8,128)S(1)} %collective-permute-done.2), channel_id=1, source_target_pairs={{0,16},{2,18},{4,20},{6,22},{8,24},{10,26},{12,28},{14,30},{16,0},... | collective-permute-start | bytes 393224 | tf_op jit(solution)/shard_map/ppermute | solution.py:10
  41.2 1.3 collective-permute-start.4
Sparse Core Ops, SparseCore 0:
  33.4 141.7 all-reduce.2
where the time goes:
time: 238 us; the launch traced here: 237 us
  waiting for transfers between devices  89.9 us (38%)
  blocking collectives  40.2 us (17%)
  other arithmetic  37.7 us (16%)
  matrix products  24.6 us (10%)
  between operations  16.6 us (7%)
  local copies, waits for them, and re-layouts  15.8 us (7%)
  starting transfers between devices  9.14 us (4%)
  loops' own time  3.37 us (1%)
    psum x1, waiting for transfers between devices, local(): lax.psum((gram, grad, local_misfit), ('gx', 'gy'))  84.2 us
    psum x1, blocking collectives, local(): lax.psum((gram, grad, local_misfit), ('gx', 'gy'))  40.2 us
    select_n x64, other arithmetic, eliminate(): return jnp.where(is_pivot, pivot_row[None, :, :], updated)  31.8 us
    dot_general x1, matrix products, local(): jnp.einsum('tb,tpq->bpq', onehot, tile_gram, precision=lax.Precision.HIGH...  10.1 us
    ppermute x5, starting transfers between devices, swapped(): lax.ppermute(value, axis, [(i, i ^ 1 << bit) for i in range(lax.axis_size...  9.1 us
    dynamic_slice x2, local copies, waits for them, and re-layouts, local(): gram = lax.dynamic_slice_in_dim(gram, leading_entry, owned, 0)  6.08 us
    dot_general x1, matrix products, local(): jnp.einsum('tpv,tqv->tpq', jacobian, jacobian, preferred_element_type=jnp...  5.77 us
    ppermute x5, waiting for transfers between devices, swapped(): lax.ppermute(value, axis, [(i, i ^ 1 << bit) for i in range(lax.axis_size...  5.65 us
  transfers between devices with their start and end apart: 6, of which 4 were waited for; matrix products, arithmetic and copies ran while one was open for 12% of the time, Pallas kernels for 0%

commit v1 on v0

--- a/solution.py
+++ b/solution.py
@@ -4,6 +4,11 @@
 from jax.sharding import PartitionSpec as P
 
 NB = 128
+
+
+def axis_by_axis(value_2, one, other):
+    partial = lax.psum(value_2, one)
+    return lax.psum(partial, other)
 
 
 def swapped(value, axis, bit):
@@ -51,7 +56,7 @@
     gram = jnp.einsum("tb,tpq->bpq", onehot, tile_gram, precision=lax.Precision.HIGHEST)
     grad = jnp.dot(onehot.T, tile_grad, precision=lax.Precision.HIGHEST)
     owned = NB // lax.axis_size("gy")
-    gram, grad, total_misfit = lax.psum((gram, grad, local_misfit), ("gx", "gy"))
+    gram, grad, total_misfit = axis_by_axis((gram, grad, local_misfit), "gy", "gx")
     leading_entry = lax.axis_index("gy") * owned
     gram = lax.dynamic_slice_in_dim(gram, leading_entry, owned, 0)
     grad = lax.dynamic_slice_in_dim(grad, leading_entry, owned, 0)

time: 238 us -> 298 us (1.25)
  blocking collectives: 40.2 us -> 84 us
  waiting for transfers between devices: 89.9 us -> 108 us
    psum x1 -> x2, blocking collectives: 40.2 us -> 84 us  [the longest x1 79.3 us: axis_by_axis(): return lax.psum(partial, other)]
    ppermute x5, waiting for transfers between devices: 5.65 us -> 26.1 us  [swapped(): lax.ppermute(value, axis, [(i, i ^ 1 << bit) for i in range(lax.axis_size...]
    psum x1 -> x2, waiting for transfers between devices: 84.2 us -> 82.1 us  [the longest x1 51.4 us: axis_by_axis(): return lax.psum(partial, other)]
  transfers between devices with their start and end apart: 6 -> 7, of which waited for: 4 -> 7; matrix products, arithmetic and copies ran while one was open for 12% -> 4% of each run, Pallas kernels for 0% -> 0%
where the time goes in v1:
time: 298 us
  waiting for transfers between devices  108 us (36%)
  blocking collectives  84 us (28%)
  other arithmetic  37.7 us (13%)
  matrix products  24.2 us (8%)
  between operations  16.6 us (6%)
  local copies, waits for them, and re-layouts  15.8 us (5%)
  starting transfers between devices  7.76 us (3%)
  loops' own time  3.37 us (1%)
    psum x1, blocking collectives, axis_by_axis(): return lax.psum(partial, other)  79.3 us
    psum x1, waiting for transfers between devices, axis_by_axis(): return lax.psum(partial, other)  51.4 us
    select_n x64, other arithmetic, eliminate(): return jnp.where(is_pivot, pivot_row[None, :, :], updated)  31.8 us
    psum x1, waiting for transfers between devices, axis_by_axis(): partial = lax.psum(value_2, one)  30.7 us
    ppermute x5, waiting for transfers between devices, swapped(): lax.ppermute(value, axis, [(i, i ^ 1 << bit) for i in range(lax.axis_size...  26.1 us
    dot_general x1, matrix products, local(): jnp.einsum('tb,tpq->bpq', onehot, tile_gram, precision=lax.Precision.HIGH...  10 us
    ppermute x5, starting transfers between devices, swapped(): lax.ppermute(value, axis, [(i, i ^ 1 << bit) for i in range(lax.axis_size...  7.5 us
    dynamic_slice x2, local copies, waits for them, and re-layouts, local(): gram = lax.dynamic_slice_in_dim(gram, leading_entry, owned, 0)  6.07 us
  transfers between devices with their start and end apart: 7, of which 7 were waited for; matrix products, arithmetic and copies ran while one was open for 4% of the time, Pallas kernels for 0%

profile of v1, /device:TPU:0, one launch (start us, length us, event | category | flops | bytes accessed | tf_op | source)
XLA Modules:
  0.0 297.6 jit_solution(11901290467826480776)
XLA Ops:
  7.2 5.8 %fusion.21 = f32[256,64,64]{2,1,0:T(8,128)S(1)} fusion(bf16[256,64,128]{2,1,0:T(8,128)(2,1)} %param.8), kind=kOutput, calls=%fused_computation.37 | convolution fusion | flops 268435456 | bytes 8388608 | tf_op jit(solution)/shard_map/tpv,tqv->tpq/dot_general | solution.py:55
  13.0 10.0 %fusion.3 = f32[128,64,64]{2,0,1:T(8,128)} fusion(f32[256,64,64]{2,1,0:T(8,128)S(1)} %fusion.21, s32[256]{0:T(256)S(1)} %copy-done.2), kind=kOutput, calls=%fused_computation.8 | convolution fusion | flops 1610645504 | bytes 6292480 | tf_op jit(solution)/shard_map/tb,tpq->bpq/dot_general | solution.py:56
  23.3 30.7 %all-reduce.5.cloned.1.call-done = f32[128,64,64]{2,0,1:T(8,128)} async-done(((f32[128,64,64]{2,0,1:T(8,128)}), f32[128,64,64]{2,0,1:T(8,128)}) %all-reduce.5.cloned.1.call-update) | async-done | bytes 2097168 | tf_op jit(solution)/shard_map/psum | solution.py:10
  54.1 1.8 collective-permute-start
  55.9 3.9 %collective-permute-done = f32[256,128]{1,0:T(8,128)S(1)} collective-permute-done((f32[256,128]{1,0:T(8,128)S(1)}, f32[256,128]{1,0:T(8,128)S(1)}, u32[]{:S(2)}, u32[]{:S(2)}) %collective-permute-start) | collective-permute-done | bytes 131104 | tf_op jit(solution)/shard_map/ppermute | solution.py:15
  59.8 1.7 collective-permute-start.1
  61.6 3.2 %collective-permute-done.1 = f32[256,128]{1,0:T(8,128)S(1)} collective-permute-done((f32[256,128]{1,0:T(8,128)S(1)}, f32[256,128]{1,0:T(8,128)S(1)}, u32[]{:S(2)}, u32[]{:S(2)}) %collective-permute-start.1) | collective-permute-done | bytes 131104 | tf_op jit(solution)/shard_map/ppermute | solution.py:15
  64.8 1.8 collective-permute-start.2
  66.8 9.3 %collective-permute-done.2 = f32[256,128]{1,0:T(8,128)S(1)} collective-permute-done((f32[256,128]{1,0:T(8,128)S(1)}, f32[256,128]{1,0:T(8,128)S(1)}, u32[]{:S(2)}, u32[]{:S(2)}) %collective-permute-start.2) | collective-permute-done | bytes 131104 | tf_op jit(solution)/shard_map/ppermute | solution.py:15
  76.1 2.2 collective-permute-start.3
  78.3 3.4 %fusion.8 = f32[256,1,128]{2,1,0:T(1,128)S(1)} fusion(bf16[256,64,128]{2,1,0:T(8,128)(2,1)} %param.8, bf16[256,64,1]{1,0,2:T(8,128)(2,1)S(1)} %fusion.5), kind=kOutput, calls=%fused_computation.16 | convolution fusion | flops 4194304 | bytes 4358144 | tf_op jit(solution)/shard_map/tpv,tp->tv/dot_general | solution.py:48
  81.7 9.0 %collective-permute-done.3 = f32[256,128]{1,0:T(8,128)S(1)} collective-permute-done((f32[256,128]{1,0:T(8,128)S(1)}, f32[256,128]{1,0:T(8,128)S(1)}, u32[]{:S(2)}, u32[]{:S(2)}) %collective-permute-start.3) | collective-permute-done | bytes 131104 | tf_op jit(solution)/shard_map/ppermute | solution.py:15
  91.4 0.7 collective-permute-done.4
  92.2 0.7 multiply_reduce_fusion
  92.9 4.5 %fusion.6 = f32[256,1,64]{2,1,0:T(1,128)S(1)} fusion(bf16[256,64,128]{2,1,0:T(8,128)(2,1)} %param.8, bf16[256,128,1]{1,0,2:T(8,128)(2,1)S(1)} %get-tuple-element.126), kind=kOutput, calls=%fused_computation.14 | convolution fusion | flops 4194304 | bytes 4325376 | tf_op jit(solution)/shard_map/tpv,tv->tp/dot_general | solution.py:54
  97.6 4.7 %all-reduce.1 = (f32[128,64]{1,0:T(8,128)S(1)}, f32[]{:T(128)}) all-reduce(f32[128,64]{1,0:T(8,128)S(1)} %fusion.10, f32[]{:T(128)} %get-tuple-element.125), channel_id=1, replica_groups=mesh['gx'=16,'gy'=2] {'gy'}, use_global_device_ids=true, to_apply=%region_2.0 | all-reduce | flops 8193 | bytes 65544 | tf_op jit(solution)/shard_map/psum | solution.py:10
  102.3 79.3 %all-reduce = (f32[128,64]{1,0:T(8,128)S(1)}, f32[]{:T(128)}) all-reduce(f32[128,64]{1,0:T(8,128)S(1)} %get-tuple-element.123, f32[]{:T(128)} %get-tuple-element.124), channel_id=1, replica_groups=mesh['gx'=16,'gy'=2] {'gx'}, use_global_device_ids=true, to_apply=%region_3.0 | all-reduce | flops 8193 | bytes 65544 | tf_op jit(solution)/shard_map/psum | solution.py:11
  181.6 1.9 copy.13
  184.2 51.4 %all-reduce.7.cloned.1.call-done = f32[128,64,64]{2,0,1:T(8,128)} async-done(((f32[128,64,64]{2,0,1:T(8,128)}), f32[128,64,64]{2,0,1:T(8,128)}) %all-reduce.7.cloned.1.call-update) | async-done | bytes 2097168 | tf_op jit(solution)/shard_map/psum | solution.py:11
  235.5 3.2 %constant_dynamic-slice_fusion.2 = f32[64,64,64]{2,0,1:T(8,128)} fusion(f32[128,64,64]{2,0,1:T(8,128)} %all-reduce.7.cloned.1.call-done, s32[]{:T(128)S(6)} %select_n.46), kind=kLoop, calls=%fused_computation.36 | loop fusion | bytes 2097156 | tf_op jit(solution)/shard_map/dynamic_slice | solution.py:61
  238.7 2.9 copy.12
  241.6 1.5 gather_fusion
  243.1 2.0 add_add_fusion
  245.1 2.0 maximum_bitcast_fusion
  247.0 2.2 copy.14
  249.2 39.3 %while.17 = (s32[]{:T(128)}, f32[64,65,64]{2,1,0:T(8,128)S(1)}, s32[]{:T(128)}, s32[]{:T(128)}, s32[]{:T(128)}, /*index=5*/s32[]{:T(128)}) while((s32[]{:T(128)}, f32[64,65,64]{2,1,0:T(8,128)S(1)}, s32[]{:T(128)}, s32[]{:T(128)}, s32[]{:T(128)}, /*index=5*/s32[]{:T(128)}) %tuple.51), condition=%wide.region_5.0_spmd.clone, body=%wide.region_4.0_spmd.clone.sunk | while | flops 802948 | bytes 2230009 | solution.py:34
  249.3 0.5 subtract_select_fusion.2
  249.9 0.5 subtract_select_fusion.2
  250.5 0.5 subtract_select_fusion.2
  251.2 0.5 subtract_select_fusion.2
  251.8 0.5 subtract_select_fusion.2
  252.4 0.5 subtract_select_fusion.2
  253.0 0.5 subtract_select_fusion.2
  253.6 0.5 subtract_select_fusion.2
  254.2 0.5 subtract_select_fusion.2
  254.8 0.5 subtract_select_fusion.2
  255.5 0.5 subtract_select_fusion.2
  256.1 0.5 subtract_select_fusion.2
  256.7 0.5 subtract_select_fusion.2
  257.3 0.5 subtract_select_fusion.2
  257.9 0.5 subtract_select_fusion.2
  258.5 0.5 subtract_select_fusion.2
  259.1 0.5 subtract_select_fusion.2
  260.4 0.5 subtract_select_fusion.2
  261.6 0.5 subtract_select_fusion.2
  262.8 0.5 subtract_select_fusion.2
  264.1 0.5 subtract_select_fusion.2
  265.3 0.5 subtract_select_fusion.2
  266.5 0.5 subtract_select_fusion.2
  267.7 0.5 subtract_select_fusion.2
  269.0 0.5 subtract_select_fusion.2
  272.0 0.5 subtract_select_fusion.2
  273.3 0.5 subtract_select_fusion.2
  274.5 0.5 subtract_select_fusion.2
  275.7 0.5 subtract_select_fusion.2
  277.0 0.5 subtract_select_fusion.2
  278.2 0.5 subtract_select_fusion.2
  279.4 0.5 subtract_select_fusion.2
  280.6 0.5 subtract_select_fusion.2
  283.7 0.5 subtract_select_fusion.2
  284.9 0.5 subtract_select_fusion.2
  286.2 0.5 subtract_select_fusion.2
  287.4 0.5 subtract_select_fusion.2
  289.0 0.7 copy.16
  (303 shorter events, 19.0 us)
Async XLA Ops:
  7.2 59.4 %copy-start = (f32[128,64]{0,1:T(8,128)S(1)}, f32[128,64]{0,1:T(8,128)}, u32[]{:S(2)}) copy-start(f32[128,64]{0,1:T(8,128)} %param.10) | copy-start | bytes 98308
  7.2 5.8 %copy-start.2 = (s32[256]{0:T(256)S(1)}, s32[256]{0:T(256)}, u32[]{:S(2)}) copy-start(s32[256]{0:T(256)} %param.9) | copy-start | bytes 3076
  7.2 46.9 %all-reduce.5.cloned.1.call-start = ((), (), s32[]{:S(2)}) async-start(), calls=%async_computation | async-start | bytes 8388608 | tf_op jit(solution)/shard_map/psum | solution.py:10
  23.1 31.0 %copy-start.1 = (f32[256,128]{1,0:T(8,128)S(1)}, f32[256,128]{1,0:T(8,128)}, u32[]{:S(2)}) copy-start(f32[256,128]{1,0:T(8,128)} %param.7) | copy-start | bytes 393220
  23.1 212.4 %all-reduce.7.cloned.1.call-start = ((), (), s32[]{:S(2)}) async-start(), calls=%async_computation.1 | async-start | bytes 8388608 | tf_op jit(solution)/shard_map/psum | solution.py:11
  54.1 5.8 %collective-permute-start = (f32[256,128]{1,0:T(8,128)S(1)}, f32[256,128]{1,0:T(8,128)S(1)}, u32[]{:S(2)}, u32[]{:S(2)}) collective-permute-start(f32[256,128]{1,0:T(8,128)S(1)} %copy-done.1), channel_id=1, source_target_pairs={{0,2},{2,0},{4,6},{6,4},{8,10},{10,8},{12,14},{14,12},{16,18},{18,... | collective-permute-start | bytes 393224 | tf_op jit(solution)/shard_map/ppermute | solution.py:15
  59.8 5.0 %collective-permute-start.1 = (f32[256,128]{1,0:T(8,128)S(1)}, f32[256,128]{1,0:T(8,128)S(1)}, u32[]{:S(2)}, u32[]{:S(2)}) collective-permute-start(f32[256,128]{1,0:T(8,128)S(1)} %collective-permute-done), channel_id=1, source_target_pairs={{0,4},{2,6},{4,0},{6,2},{8,12},{10,14},{12,8},{14,10},{16,20},{18,... | collective-permute-start | bytes 393224 | tf_op jit(solution)/shard_map/ppermute | solution.py:15
  64.8 11.3 %collective-permute-start.2 = (f32[256,128]{1,0:T(8,128)S(1)}, f32[256,128]{1,0:T(8,128)S(1)}, u32[]{:S(2)}, u32[]{:S(2)}) collective-permute-start(f32[256,128]{1,0:T(8,128)S(1)} %collective-permute-done.1), channel_id=1, source_target_pairs={{0,8},{2,10},{4,12},{6,14},{8,0},{10,2},{12,4},{14,6},{16,24},{18,... | collective-permute-start | bytes 393224 | tf_op jit(solution)/shard_map/ppermute | solution.py:15
  76.1 14.6 %collective-permute-start.3 = (f32[256,128]{1,0:T(8,128)S(1)}, f32[256,128]{1,0:T(8,128)S(1)}, u32[]{:S(2)}, u32[]{:S(2)}) collective-permute-start(f32[256,128]{1,0:T(8,128)S(1)} %collective-permute-done.2), channel_id=1, source_target_pairs={{0,16},{2,18},{4,20},{6,22},{8,24},{10,26},{12,28},{14,30},{16,0},... | collective-permute-start | bytes 393224 | tf_op jit(solution)/shard_map/ppermute | solution.py:15
  90.7 1.3 collective-permute-start.4
Sparse Core Ops, SparseCore 0:
  23.2 30.7 all-reduce.4
  59.7 175.7 all-reduce.6
